TPU v7x, 32 devices: a whole 2x2x4 slice. The times are simulated.
32 devices in a mesh: dp: 8 (over z, core), mp: 4 (over y, x).
Axes of the slice: x: 2, y: 2, z: 4, core: 2. Of those that a mesh axis runs over, the one named last changes fastest.
Arguments:
- student_in: bfloat16 [128, 6144], P(None, 'mp'), may hold values from -6 to 6
- teacher_hidden: bfloat16 [8192, 128], P('dp'), may hold values from -6 to 6
- w_up: bfloat16 [24576, 6144], P('dp', 'mp'), may hold values from -0.078125 to 0.078125
- w_down: bfloat16 [24576, 6144], P('dp', 'mp'), may hold values from -0.0390625 to 0.0390625
- w_proj: bfloat16 [8192, 6144], P('dp', 'mp'), may hold values from -0.0625 to 0.0625
Outputs:
- grad_up: float32 [24576, 6144], P('dp', 'mp')
- grad_down: float32 [24576, 6144], P('dp', 'mp')
- grad_proj: float32 [8192, 6144], P('dp', 'mp')
All inputs are finite; a program needn't handle non-finite values.
Results may differ from a plain program's by a relative error of at most 0.005.
Values may be sent and summed in bfloat16 or wider, within the bound.
No kernel may reach another device: no remote copies, remote signals or barrier semaphores. Data moves between devices by JAX's collectives and lax.ppermute only.
A program may use at most 128 MiB of HBM per device.

v0:
```python
import math
import jax
import jax.numpy as jnp
from jax import lax
from jax.sharding import PartitionSpec as P


def contract_first(left, right):
    return lax.dot_general(
        left, right, (((0,), (0,)), ((), ())), preferred_element_type=jnp.float32
    )


def contract_last(left, right):
    return lax.dot_general(
        left, right, (((1,), (1,)), ((), ())), preferred_element_type=jnp.float32
    )


def body(student_in, teacher_hidden, w_up, w_down, w_proj):
    tokens_all = student_in.shape[0]
    partial_pre = contract_last(w_up, student_in)
    pre = lax.psum(partial_pre, "mp")
    active = jnp.maximum(pre, 0.0)
    hidden = (active * active).astype(jnp.bfloat16)
    student_part = contract_first(hidden, w_down)
    target_part = contract_first(teacher_hidden, w_proj)
    residual = lax.psum_scatter(student_part - target_part, "dp", scatter_dimension=0, tiled=True)
    d_local = (residual * (1.0 / math.sqrt(tokens_all))).astype(jnp.bfloat16)
    piece = lax.all_gather(d_local, "dp", axis=0, tiled=True)
    proj_acc = jnp.zeros(w_proj.shape, jnp.float32)
    down_acc = jnp.dot(hidden, piece, preferred_element_type=jnp.float32)
    proj_acc = proj_acc - jnp.dot(teacher_hidden, piece, preferred_element_type=jnp.float32)
    grad_cols = contract_last(w_down, piece)
    d_hidden = lax.psum(grad_cols, "mp")
    d_pre = (d_hidden * (2.0 * active)).astype(jnp.bfloat16)
    grad_up = jnp.dot(d_pre, student_in, preferred_element_type=jnp.float32)
    return (grad_up, down_acc, proj_acc)


def solution(mesh):
    return jax.shard_map(
        body,
        mesh=mesh,
        in_specs=(P(None, "mp"), P("dp", None), P("dp", "mp"), P("dp", "mp"), P("dp", "mp")),
        out_specs=(P("dp", "mp"), P("dp", "mp"), P("dp", "mp")),
        check_vma=False,
    )
```

profile of v0, /device:TPU:0, one launch (start us, length us, event | category | flops | bytes accessed | tf_op | source)
XLA Modules:
  0.0 216.5 jit_solution(6784596743819639396)
XLA Ops:
  7.2 0.0 copy-start
  7.2 0.0 all-reduce.3.cloned.1.call-start
  7.2 7.6 %fusion.9 = f32[3072,128]{1,0:T(8,128)} fusion(bf16[3072,1536]{1,0:T(8,128)(2,1)} %param.7, bf16[128,1536]{1,0:T(8,128)(2,1)} %param.5), kind=kOutput, calls=%fused_computation.15 | convolution fusion | flops 1207959552 | bytes 11403264 | tf_op jit(solution)/shard_map/dot_general | solution.py:15
  14.8 0.0 all-reduce.3.cloned.1.call-update
  14.8 0.0 copy-start.4
  14.8 0.0 reduce-scatter.2.cloned.1.call-start
  14.9 63.5 %all-reduce.3.cloned.1.call-done = f32[3072,128]{1,0:T(8,128)} async-done(((f32[3072,128]{1,0:T(8,128)}), f32[3072,128]{1,0:T(8,128)}) %all-reduce.3.cloned.1.call-update) | async-done | bytes 1572880 | tf_op jit(solution)/shard_map/psum | solution.py:23
  78.4 5.6 %fusion.4 = f32[128,1536]{1,0:T(8,128)S(1)} fusion(bf16[3072,1536]{1,0:T(8,128)(2,1)} %param.8, f32[3072,128]{1,0:T(8,128)} %all-reduce.3.cloned.1.call-done), kind=kOutput, calls=%fused_computation.9 | convolution fusion | flops 1209139200 | bytes 11796480 | tf_op jit(solution)/shard_map/dot_general | solution.py:9
  84.1 0.0 copy-done
  84.1 0.0 copy-done.4
  84.1 1.5 convolution_subtract_fusion
  85.6 0.0 reduce-scatter.2.cloned.1.call-update
  85.6 0.0 all-reduce.5.cloned.1.call-start
  85.6 31.9 %reduce-scatter.2.cloned.1.call-done = f32[16,1536]{1,0:T(8,128)} async-done(((f32[128,1536]{1,0:T(8,128)}), f32[16,1536]{1,0:T(8,128)}) %reduce-scatter.2.cloned.1.call-update) | async-done | bytes 98320 | tf_op jit(solution)/shard_map/reduce_scatter | solution.py:28
  117.6 0.9 multiply_convert_fusion.5
  118.5 14.5 %all_gather.3 = bf16[128,1536]{1,0:T(8,128)(2,1)S(1)} all-gather(bf16[16,1536]{1,0:T(8,128)(2,1)S(1)} %multiply_convert_fusion.5), channel_id=1, replica_groups=mesh['dp'=8,'mp'=4] {'dp'}, dimensions={0}, use_global_device_ids=true | all-gather | bytes 442368 | tf_op jit(solution)/shard_map/all_gather | solution.py:30
  132.9 7.4 %convolution_bitcast_fusion = f32[3072,128]{1,0:T(8,128)} fusion(bf16[128,1536]{1,0:T(8,128)(2,1)S(1)} %all_gather.3, bf16[3072,1536]{1,0:T(8,128)(2,1)} %param.8), kind=kOutput, calls=%fused_computation.1 | convolution fusion | flops 1207959552 | bytes 11403264 | tf_op jit(solution)/shard_map/dot_general | solution.py:15
  140.4 0.0 all-reduce.5.cloned.1.call-update
  140.4 3.7 %subtract_bitcast_fusion = f32[1024,1536]{0,1:T(8,128)} fusion(bf16[128,1536]{1,0:T(8,128)(2,1)S(1)} %all_gather.3, bf16[1024,128]{1,0:T(8,128)(2,1)S(1)} %copy-done.4), kind=kOutput, calls=%fused_computation | convolution fusion | flops 404226048 | bytes 6946816 | tf_op jit(solution)/shard_map/dot_general | solution.py:33
  144.1 0.0 copy-start.2
  144.1 6.7 %copy.8 = f32[1024,1536]{1,0:T(8,128)} copy(f32[1024,1536]{0,1:T(8,128)} %subtract_bitcast_fusion) | data formatting | bytes 12582912
  150.9 0.0 copy-done.2
  150.9 0.0 copy-start.3
  150.9 8.2 %fusion.3 = f32[3072,1536]{1,0:T(8,128)} fusion(bf16[128,1536]{1,0:T(8,128)(2,1)S(1)} %all_gather.3, f32[3072,128]{1,0:T(8,128)S(1)} %copy-done.2), kind=kOutput, calls=%fused_computation.8 | convolution fusion | flops 1209139200 | bytes 20840448 | tf_op jit(solution)/shard_map/dot_general | solution.py:32
  159.1 40.6 %all-reduce.5.cloned.1.call-done = f32[3072,128]{1,0:T(8,128)} async-done(((f32[3072,128]{1,0:T(8,128)}), f32[3072,128]{1,0:T(8,128)}) %all-reduce.5.cloned.1.call-update) | async-done | bytes 1572880 | tf_op jit(solution)/shard_map/psum | solution.py:35
  199.7 0.0 copy-done.3
  199.7 0.0 copy-start.1
  199.7 10.3 %fusion = f32[3072,1536]{1,0:T(8,128)} fusion(bf16[128,1536]{1,0:T(8,128)(2,1)S(1)} %copy-done.3, f32[3072,128]{1,0:T(8,128)} %all-reduce.5.cloned.1.call-done, f32[3072,128]{1,0:T(8,128)} %all-reduce.3.cloned.1.call-done), kind=kOutput, calls=%fused_computation.5 | convolution fusion | flops 1209532416 | bytes 22413312 | tf_op jit(solution)/shard_map/dot_general | solution.py:37
  210.0 0.0 copy-done.1
Async XLA Ops:
  7.2 76.9 %copy-start = (bf16[1024,1536]{1,0:T(8,128)(2,1)S(1)}, bf16[1024,1536]{1,0:T(8,128)(2,1)}, u32[]{:S(2)}) copy-start(bf16[1024,1536]{1,0:T(8,128)(2,1)} %param.9) | copy-start | bytes 9437188
  7.2 71.3 %all-reduce.3.cloned.1.call-start = ((), (), s32[]{:S(2)}) async-start(), calls=%async_computation.1 | async-start | bytes 3145728 | tf_op jit(solution)/shard_map/psum | solution.py:23
  14.8 69.2 %copy-start.4 = (bf16[1024,128]{1,0:T(8,128)(2,1)S(1)}, bf16[1024,128]{1,0:T(8,128)(2,1)}, u32[]{:S(2)}) copy-start(bf16[1024,128]{1,0:T(8,128)(2,1)} %param.6) | copy-start | bytes 786436
  14.8 102.7 %reduce-scatter.2.cloned.1.call-start = ((), (), s32[]{:S(2)}) async-start(), calls=%async_computation.2 | async-start | bytes 884736 | tf_op jit(solution)/shard_map/reduce_scatter | solution.py:28
  85.6 114.1 %all-reduce.5.cloned.1.call-start = ((), (), s32[]{:S(2)}) async-start(), calls=%async_computation.3 | async-start | bytes 3145728 | tf_op jit(solution)/shard_map/psum | solution.py:35
  144.1 6.7 %copy-start.2 = (f32[3072,128]{1,0:T(8,128)S(1)}, f32[3072,128]{1,0:T(8,128)}, u32[]{:S(2)}) copy-start(f32[3072,128]{1,0:T(8,128)} %all-reduce.3.cloned.1.call-done) | copy-start | bytes 4718596
  150.9 48.8 %copy-start.3 = (bf16[128,1536]{1,0:T(8,128)(2,1)S(1)}, bf16[128,1536]{1,0:T(8,128)(2,1)}, u32[]{:S(2)}) copy-start(bf16[128,1536]{1,0:T(8,128)(2,1)} %param.5) | copy-start | bytes 1179652
  199.7 10.3 %copy-start.1 = (bf16[1024,1536]{1,0:T(8,128)(2,1)S(1)}, bf16[1024,1536]{1,0:T(8,128)(2,1)}, u32[]{:S(2)}) copy-start(bf16[1024,1536]{1,0:T(8,128)(2,1)} %param.9) | copy-start | bytes 9437188
Sparse Core Ops, SparseCore 0:
  15.0 63.4 all-reduce.2
  85.7 31.8 reduce-scatter.1
  140.5 59.1 all-reduce.4
where the time goes:
time: 217 us; the launch traced here: 216 us
  waiting for transfers between devices  136 us (63%)
  matrix products  44.3 us (20%)
  blocking collectives  14.5 us (7%)
  between operations  13.8 us (6%)
  local copies, waits for them, and re-layouts  6.75 us (3%)
    psum x1, waiting for transfers between devices, body(): pre = lax.psum(partial_pre, 'mp')  63.5 us
    psum x1, waiting for transfers between devices, body(): d_hidden = lax.psum(grad_cols, 'mp')  40.6 us
    reduce_scatter x1, waiting for transfers between devices, body(): lax.psum_scatter(student_part - target_part, 'dp', scatter_dimension=0, t...  31.9 us
    dot_general x2, matrix products, contract_last(): lax.dot_general(left, right, (((1,), (1,)), ((), ())), preferred_element_...  15 us
    all_gather x1, blocking collectives, body(): piece = lax.all_gather(d_local, 'dp', axis=0, tiled=True)  14.5 us
    dot_general x1, matrix products, body(): grad_up = jnp.dot(d_pre, student_in, preferred_element_type=jnp.float32)  10.3 us
    dot_general x1, matrix products, body(): down_acc = jnp.dot(hidden, piece, preferred_element_type=jnp.float32)  8.22 us
    dot_general x2, matrix products, contract_first(): lax.dot_general(left, right, (((0,), (0,)), ((), ())), preferred_element_...  7.09 us
  transfers between devices with their start and end apart: 3, of which 3 were waited for; matrix products, arithmetic and copies ran while one was open for 9% of the time, Pallas kernels for 0%

commit v1 on v0

--- a/solution.py
+++ b/solution.py
@@ -20,7 +20,8 @@
 def body(student_in, teacher_hidden, w_up, w_down, w_proj):
     tokens_all = student_in.shape[0]
     partial_pre = contract_last(w_up, student_in)
-    pre = lax.psum(partial_pre, "mp")
+    pieces = lax.all_gather(partial_pre, "mp")
+    pre = jnp.sum(pieces, axis=0)
     active = jnp.maximum(pre, 0.0)
     hidden = (active * active).astype(jnp.bfloat16)
     student_part = contract_first(hidden, w_down)

time: 217 us -> 231 us (1.065)
  waiting for transfers between devices: 136 us -> 146 us
  other arithmetic: 0.9 us -> 5.34 us
    all_gather x0 -> x1, waiting for transfers between devices: none -> 72.9 us  [body(): pieces = lax.all_gather(partial_pre, 'mp')]
    psum x1 -> x0, waiting for transfers between devices: 63.5 us -> none  [body(): pre = lax.psum(partial_pre, 'mp')]
    reduce_sum x0 -> x1, other arithmetic: none -> 4.44 us  [body(): pre = jnp.sum(pieces, axis=0)]
  transfers between devices with their start and end apart: 3 -> 3, of which waited for: 3 -> 3; matrix products, arithmetic and copies ran while one was open for 9% -> 8% of each run, Pallas kernels for 0% -> 0%
where the time goes in v1:
time: 231 us; the launch traced here: 230 us
  waiting for transfers between devices  146 us (63%)
  matrix products  44.3 us (19%)
  blocking collectives  14.5 us (6%)
  between operations  13.8 us (6%)
  local copies, waits for them, and re-layouts  6.82 us (3%)
  other arithmetic  5.34 us (2%)
    all_gather x1, waiting for transfers between devices, body(): pieces = lax.all_gather(partial_pre, 'mp')  72.9 us
    psum x1, waiting for transfers between devices, body(): d_hidden = lax.psum(grad_cols, 'mp')  40.8 us
    reduce_scatter x1, waiting for transfers between devices, body(): lax.psum_scatter(student_part - target_part, 'dp', scatter_dimension=0, t...  31.9 us
    dot_general x2, matrix products, contract_last(): lax.dot_general(left, right, (((1,), (1,)), ((), ())), preferred_element_...  15 us
    all_gather x1, blocking collectives, body(): piece = lax.all_gather(d_local, 'dp', axis=0, tiled=True)  14.5 us
    dot_general x1, matrix products, body(): grad_up = jnp.dot(d_pre, student_in, preferred_element_type=jnp.float32)  10.3 us
    dot_general x1, matrix products, body(): down_acc = jnp.dot(hidden, piece, preferred_element_type=jnp.float32)  8.22 us
    dot_general x2, matrix products, contract_first(): lax.dot_general(left, right, (((0,), (0,)), ((), ())), preferred_element_...  7.12 us
  transfers between devices with their start and end apart: 3, of which 3 were waited for; matrix products, arithmetic and copies ran while one was open for 8% of the time, Pallas kernels for 0%

profile of v1, /device:TPU:0, one launch (start us, length us, event | category | flops | bytes accessed | tf_op | source)
XLA Modules:
  0.0 230.5 jit_solution(11348924547978161862)
XLA Ops:
  7.2 0.0 copy-start
  7.2 0.0 all-gather.3.cloned.1.call-start
  7.2 7.6 %fusion.9 = f32[3072,128]{1,0:T(8,128)} fusion(bf16[3072,1536]{1,0:T(8,128)(2,1)} %param.7, bf16[128,1536]{1,0:T(8,128)(2,1)} %param.5), kind=kOutput, calls=%fused_computation.15 | convolution fusion | flops 1207959552 | bytes 11403264 | tf_op jit(solution)/shard_map/dot_general | solution.py:15
  14.8 0.0 all-gather.3.cloned.1.call-update
  14.8 0.0 reduce-scatter.2.cloned.1.call-start
  14.9 72.9 %all-gather.3.cloned.1.call-done = f32[12288,128]{1,0:T(8,128)} async-done(((f32[3072,128]{1,0:T(8,128)}), f32[12288,128]{1,0:T(8,128)}) %all-gather.3.cloned.1.call-update) | async-done | bytes 6291472 | tf_op jit(solution)/shard_map/all_gather | solution.py:23
  87.7 4.4 %reduce_sum.9 = f32[3072,128]{1,0:T(8,128)} reduce(f32[4,3072,128]{2,1,0:T(8,128)} %bitcast.16, f32[]{:T(128)} %constant.3.clone.1), dimensions={0}, to_apply=%region_0.0 | reduce | flops 1179648 | bytes 7864324 | tf_op jit(solution)/shard_map/reduce_sum | solution.py:24
  92.2 0.0 copy-start.4
  92.2 5.6 %fusion.4 = f32[128,1536]{1,0:T(8,128)S(1)} fusion(bf16[3072,1536]{1,0:T(8,128)(2,1)} %param.8, f32[3072,128]{1,0:T(8,128)} %reduce_sum.9), kind=kOutput, calls=%fused_computation.9 | convolution fusion | flops 1209139200 | bytes 11796480 | tf_op jit(solution)/shard_map/dot_general | solution.py:9
  97.8 0.0 copy-done
  97.8 0.0 copy-done.4
  97.9 1.5 convolution_subtract_fusion
  99.3 0.0 reduce-scatter.2.cloned.1.call-update
  99.4 0.0 all-reduce.2.cloned.1.call-start
  99.4 31.9 %reduce-scatter.2.cloned.1.call-done = f32[16,1536]{1,0:T(8,128)} async-done(((f32[128,1536]{1,0:T(8,128)}), f32[16,1536]{1,0:T(8,128)}) %reduce-scatter.2.cloned.1.call-update) | async-done | bytes 98320 | tf_op jit(solution)/shard_map/reduce_scatter | solution.py:29
  131.4 0.9 multiply_convert_fusion.5
  132.3 14.5 %all_gather.11 = bf16[128,1536]{1,0:T(8,128)(2,1)S(1)} all-gather(bf16[16,1536]{1,0:T(8,128)(2,1)S(1)} %multiply_convert_fusion.5), channel_id=1, replica_groups=mesh['dp'=8,'mp'=4] {'dp'}, dimensions={0}, use_global_device_ids=true | all-gather | bytes 442368 | tf_op jit(solution)/shard_map/all_gather | solution.py:31
  146.7 7.4 %convolution_bitcast_fusion = f32[3072,128]{1,0:T(8,128)} fusion(bf16[128,1536]{1,0:T(8,128)(2,1)S(1)} %all_gather.11, bf16[3072,1536]{1,0:T(8,128)(2,1)} %param.8), kind=kOutput, calls=%fused_computation.1 | convolution fusion | flops 1207959552 | bytes 11403264 | tf_op jit(solution)/shard_map/dot_general | solution.py:15
  154.2 0.0 all-reduce.2.cloned.1.call-update
  154.2 3.7 %subtract_bitcast_fusion = f32[1024,1536]{0,1:T(8,128)} fusion(bf16[128,1536]{1,0:T(8,128)(2,1)S(1)} %all_gather.11, bf16[1024,128]{1,0:T(8,128)(2,1)S(1)} %copy-done.4), kind=kOutput, calls=%fused_computation | convolution fusion | flops 404226048 | bytes 6946816 | tf_op jit(solution)/shard_map/dot_general | solution.py:34
  157.9 0.0 copy-start.2
  157.9 6.8 %copy.8 = f32[1024,1536]{1,0:T(8,128)} copy(f32[1024,1536]{0,1:T(8,128)} %subtract_bitcast_fusion) | data formatting | bytes 12582912
  164.7 0.0 copy-done.2
  164.7 0.0 copy-start.3
  164.7 8.2 %fusion.3 = f32[3072,1536]{1,0:T(8,128)} fusion(bf16[128,1536]{1,0:T(8,128)(2,1)S(1)} %all_gather.11, f32[3072,128]{1,0:T(8,128)S(1)} %copy-done.2), kind=kOutput, calls=%fused_computation.8 | convolution fusion | flops 1209139200 | bytes 20840448 | tf_op jit(solution)/shard_map/dot_general | solution.py:33
  172.9 40.8 %all-reduce.2.cloned.1.call-done = f32[3072,128]{1,0:T(8,128)} async-done(((f32[3072,128]{1,0:T(8,128)}), f32[3072,128]{1,0:T(8,128)}) %all-reduce.2.cloned.1.call-update) | async-done | bytes 1572880 | tf_op jit(solution)/shard_map/psum | solution.py:36
  213.7 0.0 copy-done.3
  213.7 0.0 copy-start.1
  213.7 10.3 %fusion = f32[3072,1536]{1,0:T(8,128)} fusion(bf16[128,1536]{1,0:T(8,128)(2,1)S(1)} %copy-done.3, f32[3072,128]{1,0:T(8,128)} %all-reduce.2.cloned.1.call-done, f32[3072,128]{1,0:T(8,128)} %reduce_sum.9), kind=kOutput, calls=%fused_computation.5 | convolution fusion | flops 1209532416 | bytes 22413312 | tf_op jit(solution)/shard_map/dot_general | solution.py:38
  223.9 0.0 copy-done.1
Async XLA Ops:
  7.2 90.7 %copy-start = (bf16[1024,1536]{1,0:T(8,128)(2,1)S(1)}, bf16[1024,1536]{1,0:T(8,128)(2,1)}, u32[]{:S(2)}) copy-start(bf16[1024,1536]{1,0:T(8,128)(2,1)} %param.9) | copy-start | bytes 9437188
  7.2 80.6 %all-gather.3.cloned.1.call-start = ((), (), s32[]{:S(2)}) async-start(), calls=%async_computation.3 | async-start | bytes 7864320 | tf_op jit(solution)/shard_map/all_gather | solution.py:23
  14.8 116.5 %reduce-scatter.2.cloned.1.call-start = ((), (), s32[]{:S(2)}) async-start(), calls=%async_computation.1 | async-start | bytes 884736 | tf_op jit(solution)/shard_map/reduce_scatter | solution.py:29
  92.2 5.7 %copy-start.4 = (bf16[1024,128]{1,0:T(8,128)(2,1)S(1)}, bf16[1024,128]{1,0:T(8,128)(2,1)}, u32[]{:S(2)}) copy-start(bf16[1024,128]{1,0:T(8,128)(2,1)} %param.6) | copy-start | bytes 786436
  99.4 114.3 %all-reduce.2.cloned.1.call-start = ((), (), s32[]{:S(2)}) async-start(), calls=%async_computation.2 | async-start | bytes 3145728 | tf_op jit(solution)/shard_map/psum | solution.py:36
  157.9 6.8 %copy-start.2 = (f32[3072,128]{1,0:T(8,128)S(1)}, f32[3072,128]{1,0:T(8,128)}, u32[]{:S(2)}) copy-start(f32[3072,128]{1,0:T(8,128)} %reduce_sum.9) | copy-start | bytes 4718596
  164.7 49.0 %copy-start.3 = (bf16[128,1536]{1,0:T(8,128)(2,1)S(1)}, bf16[128,1536]{1,0:T(8,128)(2,1)}, u32[]{:S(2)}) copy-start(bf16[128,1536]{1,0:T(8,128)(2,1)} %param.5) | copy-start | bytes 1179652
  213.7 10.3 %copy-start.1 = (bf16[1024,1536]{1,0:T(8,128)(2,1)S(1)}, bf16[1024,1536]{1,0:T(8,128)(2,1)}, u32[]{:S(2)}) copy-start(bf16[1024,1536]{1,0:T(8,128)(2,1)} %param.9) | copy-start | bytes 9437188
Sparse Core Ops, SparseCore 0:
  15.0 72.7 all-gather.2
  99.5 31.8 reduce-scatter.1
  154.3 59.3 all-reduce.1
